TPU v7x, 32 devices: a whole 2x2x4 slice. The times are simulated.
32 devices in a mesh: ctx: 8 (over y, x, core), head: 4 (over z).
Axes of the slice: x: 2, y: 2, z: 4, core: 2. Of those that a mesh axis runs over, the one named last changes fastest.
Arguments:
- queries: bfloat16 [4096, 4096], P('ctx', 'head'), may hold values from -8 to 8
- keys: bfloat16 [4096, 1024], P('ctx', 'head'), may hold values from -8 to 8
- values: bfloat16 [4096, 1024], P('ctx', 'head'), may hold values from -6 to 6
- lengths: int32 [16], replicated, may hold values from 1 to 1024, 4096 in all
- out_weight: bfloat16 [4096, 4096], P(None, 'head'), may hold values from -0.09375 to 0.09375
Outputs:
- mixed: bfloat16 [4096, 4096], P('ctx', 'head')
Inputs may be any that keep to these rules, and one draw needn't show every extreme that they name: `lengths`: each document holds at least one token and one holds exactly 1024; they sum to 4096.
All inputs are finite; a program needn't handle non-finite values.
Results may differ from a plain program's by a relative error of at most 0.0085.
Values may be sent and summed in bfloat16 or wider, within the bound.
No kernel may reach another device: no remote copies, remote signals or barrier semaphores. Data moves between devices by JAX's collectives and lax.ppermute only.
A program may use at most 64 MiB of HBM per device.

v0:
```python
import jax
import jax.numpy as jnp
from jax import lax
from jax.sharding import PartitionSpec as P

HEAD_SIZE = 128


def shifted(shard, axis, by):
    peers = lax.axis_size(axis)
    pairs = [(i, i + by) for i in range(peers) if 0 <= i + by < peers]
    return lax.ppermute(shard, axis, pairs)


def doc_labels(lengths, positions):
    boundary = jnp.cumsum(lengths)
    return jnp.sum((boundary[None, :] <= positions[:, None]).astype(jnp.int32), axis=1) + 1


def attend(softmax_state, grouped_queries, labels, key_block, value_block, key_labels, causal):
    tok_local = grouped_queries.shape[0]
    kv_local = key_block.shape[1] // HEAD_SIZE
    keyed_rows = key_block.reshape(tok_local, kv_local, HEAD_SIZE)
    valued_rows = value_block.reshape(tok_local, kv_local, HEAD_SIZE)
    scores = jnp.einsum(
        "tkgd,skd->kgts", grouped_queries, keyed_rows, preferred_element_type=jnp.float32
    ) * HEAD_SIZE ** (-0.5)
    allowed = labels[:, None] == key_labels[None, :]
    if causal:
        allowed = allowed & jnp.tril(jnp.ones((tok_local, tok_local), dtype=bool))
    scores = jnp.where(allowed, scores, -1e30)
    run_max, run_total, numer = softmax_state
    new_max = jnp.maximum(run_max, jnp.max(scores, axis=-1))
    factor = jnp.exp(run_max - new_max)
    weights = jnp.exp(scores - new_max[..., None])
    run_total = run_total * factor + jnp.sum(weights, axis=-1)
    numer = numer * factor[..., None] + jnp.einsum(
        "kgts,skd->kgtd",
        weights.astype(jnp.bfloat16),
        valued_rows,
        preferred_element_type=jnp.float32,
    )
    return (new_max, run_total, numer)


def shards(queries, keys, values, lengths, out_weight):
    tok_local = queries.shape[0]
    kv_local = keys.shape[1] // HEAD_SIZE
    query_group_size = queries.shape[1] // keys.shape[1]
    positions = lax.axis_index("ctx") * tok_local + jnp.arange(tok_local, dtype=jnp.int32)
    labels = doc_labels(lengths, positions)
    grouped_queries = queries.reshape(tok_local, kv_local, query_group_size, HEAD_SIZE)
    softmax_state = (
        jnp.full((kv_local, query_group_size, tok_local), -1e30, jnp.float32),
        jnp.zeros((kv_local, query_group_size, tok_local), jnp.float32),
        jnp.zeros((kv_local, query_group_size, tok_local, HEAD_SIZE), jnp.float32),
    )
    softmax_state = attend(softmax_state, grouped_queries, labels, keys, values, labels, True)
    reach_shards = lax.axis_size("ctx") // 4

    def visit(state_now, carried):
        return (
            attend(state_now, grouped_queries, labels, carried[0], carried[1], carried[2], False),
            None,
        )

    def turn_step(turn_index, carry):
        state_now, carried = carry
        carried = shifted((carried[0], carried[1], carried[2]), "ctx", 1)
        return (visit(state_now, carried)[0], carried)

    softmax_state, unused = lax.fori_loop(
        0, reach_shards, turn_step, (softmax_state, (keys, values, labels))
    )
    run_max, run_total, numer = softmax_state
    attended = numer / run_total[..., None]
    attended = (
        jnp.transpose(attended, (2, 0, 1, 3))
        .reshape(tok_local, queries.shape[1])
        .astype(jnp.bfloat16)
    )
    mixed = jnp.dot(
        lax.all_gather(attended, "head", axis=1, tiled=True),
        out_weight,
        preferred_element_type=jnp.float32,
    )
    return mixed.astype(jnp.bfloat16)


def solution(mesh):
    return jax.shard_map(
        shards,
        mesh=mesh,
        in_specs=(P("ctx", "head"), P("ctx", "head"), P("ctx", "head"), P(), P(None, "head")),
        out_specs=P("ctx", "head"),
        check_vma=False,
    )
```

profile of v0, /device:TPU:0, one launch (start us, length us, event | category | flops | bytes accessed | tf_op | source)
XLA Modules:
  0.0 160.9 jit_solution(7699841117121816501)
XLA Ops:
  6.5 0.0 all-gather.2.cloned.1.call-start
  6.5 0.7 copy.27
  7.3 0.1 reduce
  7.4 0.1 convert_reduce_fusion
  7.5 0.2 fusion.19
  7.7 1.0 reshape.65
  8.8 1.1 copy.33
  9.9 1.0 reshape.67
  10.9 1.1 copy.34
  12.0 1.5 copy.28
  13.5 0.7 copy.35
  14.2 1.6 fusion.12
  15.8 1.7 %fusion.11 = f32[2,4,512]{2,1,0:T(4,128)S(1)} fusion(f32[2,512,512,4]{2,1,3,0:T(8,128)S(1)} %get-tuple-element.98, f32[2,4,512]{2,1,0:T(4,128)S(1)} %broadcast_maximum_fusion, pred[512,512]{0,1:T(8,128)(4,1)S(1)} %fusion.19), kind=kLoop, calls=%fused_computation.16 | loop fusion | flops 8384512 | bytes 8683520 | tf_op jit(solution)/shard_map/reduce_sum | solution.py:36
  17.5 3.9 %fusion.16 = f32[2,4,512,128]{3,2,1,0:T(8,128)} fusion(f32[2,512,512,4]{2,1,3,0:T(8,128)S(1)} %get-tuple-element.98, f32[2,4,512]{2,1,0:T(4,128)S(1)} %broadcast_maximum_fusion, pred[512,512]{0,1:T(8,128)(4,1)S(1)} %fusion.19, f32[2,4,512]{2,1,0:T(4,128)S(1)} %get-tuple-element.95, bf16[512,2,128,1]{2,1,0,3:T(2,128)(2,1)S(1)} %bitcast.91), kind=kOutput, calls=%fused_computation.21 | convolution fusion | flops 545783808 | bytes 11042816 | tf_op jit(solution)/shard_map/kgts,skd->kgtd/dot_general | solution.py:37
  21.4 35.6 %while.20 = (s32[]{:T(128)}, f32[2,4,512]{2,1,0:T(4,128)S(1)}, f32[2,4,512]{2,1,0:T(4,128)S(1)}, f32[2,4,512,128]{3,2,1,0:T(8,128)}, bf16[512,256]{0,1:T(8,128)(...) while((s32[]{:T(128)}, f32[2,4,512]{2,1,0:T(4,128)S(1)}, ...), condition=%wide.region_7.8_spmd, body=%wide.region_4.7_spmd.sunk | while | flops 1098129408 | bytes 52183316 | solution.py:72
  21.4 2.4 %collective-permute-start.1 = (bf16[512,256]{0,1:T(8,128)(2,1)S(1)}, bf16[512,256]{0,1:T(8,128)(2,1)S(1)}, u32[]{:S(2)}, u32[]{:S(2)}) collective-permute-start(bf16[512,256]{0,1:T(8,128)(2,1)S(1)} %get-tuple-element.180), channel_id=1, source_target_pairs={{0,4},{4,8},{8,12},{12,16},{16,20},{20,24},{24,28},{1,5},{5,9},{9,... | collective-permute-start | bytes 786440 | tf_op jit(solution)/shard_map/while/body/eval_jaxpr/ppermute | solution.py:12
  23.8 4.5 %collective-permute-start = (s32[512]{0:T(512)S(1)}, s32[512]{0:T(512)S(1)}, u32[]{:S(2)}, u32[]{:S(2)}) collective-permute-start(s32[512]{0:T(512)S(1)} %get-tuple-element.182), channel_id=1, source_target_pairs={{0,4},{4,8},{8,12},{12,16},{16,20},{20,24},{24,28},{1,5},{5,9},{9,... | collective-permute-start | bytes 6152 | tf_op jit(solution)/shard_map/while/body/eval_jaxpr/ppermute | solution.py:12
  28.3 1.9 %collective-permute-start.2 = (bf16[512,256]{0,1:T(8,128)(2,1)S(1)}, bf16[512,256]{0,1:T(8,128)(2,1)S(1)}, u32[]{:S(2)}, u32[]{:S(2)}) collective-permute-start(bf16[512,256]{0,1:T(8,128)(2,1)S(1)} %get-tuple-element.181), channel_id=1, source_target_pairs={{0,4},{4,8},{8,12},{12,16},{16,20},{20,24},{24,28},{1,5},{5,9},{9,... | collective-permute-start | bytes 786440 | tf_op jit(solution)/shard_map/while/body/eval_jaxpr/ppermute | solution.py:12
  30.2 0.0 collective-permute-done
  30.3 0.2 broadcast_compare_fusion.2
  30.5 0.0 collective-permute-done.1
  30.5 0.0 copy-start
  30.5 2.0 %fusion.42 = (f32[2,4,512]{2,1,0:T(4,128)S(1)}, f32[2,512,512,4]{2,1,3,0:T(8,128)S(1)}) fusion(pred[512,512]{0,1:T(8,128)(4,1)S(1)} %broadcast_compare_fusion.2, bf16[512,2,128,1]{0,2,3,1:T(8,128)(2,1)S(1)} %bitcast.79, bf16[512,2,4,128]{3,0,2,1:T(8,128)(2,1)S(1)} %get-tuple-element.194), kind=kOutput, calls=%fused_computation.4.clone.1 | convolution fusion | flops 543158272 | bytes 9977856 | tf_op jit(solution)/shard_map/while/body/eval_jaxpr/tkgd,skd->kgts/dot_general | solution.py:25
  32.6 1.7 %fusion.43 = f32[2,4,512]{2,1,0:T(4,128)S(1)} fusion(f32[2,512,512,4]{2,1,3,0:T(8,128)S(1)} %get-tuple-element.163, f32[2,4,512]{2,1,0:T(4,128)S(1)} %max.4, pred[512,512]{0,1:T(8,128)(4,1)S(1)} %broadcast_compare_fusion.2), kind=kLoop, calls=%fused_computation.3.clone.1 | loop fusion | flops 8384512 | bytes 8683520 | tf_op jit(solution)/shard_map/while/body/eval_jaxpr/reduce_sum | solution.py:36
  34.3 0.0 collective-permute-done.2
  34.3 0.0 copy-done
  34.4 3.4 %multiply_add_fusion.5 = f32[2,4,512,128]{3,2,1,0:T(8,128)S(1)} fusion(f32[2,4,512,128]{3,2,1,0:T(8,128)S(1)} %copy-done, bf16[512,2,128,1]{0,2,3,1:T(8,128)(2,1)S(1)} %bitcast.83, f32[2,512,512,4]{2,1,3,0:T(8,128)S(1)} %get-tuple-element.163, f32[2,4,512]{2,1,0:T(4,128)S(1)} %max.4, pred[512,512]{0,1:T(8,128)(4,1)S(1)} %broadcast_compare_fusion.2, ...), kind=kOutput, calls=%fused_computation.7.clone.1 | convolution fusion | flops 546308096 | bytes 13139968 | tf_op jit(solution)/shard_map/while/body/eval_jaxpr/kgts,skd->kgtd/dot_general | solution.py:37
  37.8 0.0 copy-start.1
  37.8 1.3 copy-done.1
  39.1 3.5 %collective-permute-start.1 = (bf16[512,256]{0,1:T(8,128)(2,1)S(1)}, bf16[512,256]{0,1:T(8,128)(2,1)S(1)}, u32[]{:S(2)}, u32[]{:S(2)}) collective-permute-start(bf16[512,256]{0,1:T(8,128)(2,1)S(1)} %get-tuple-element.180), channel_id=1, source_target_pairs={{0,4},{4,8},{8,12},{12,16},{16,20},{20,24},{24,28},{1,5},{5,9},{9,... | collective-permute-start | bytes 786440 | tf_op jit(solution)/shard_map/while/body/eval_jaxpr/ppermute | solution.py:12
  42.6 3.5 %collective-permute-start = (s32[512]{0:T(512)S(1)}, s32[512]{0:T(512)S(1)}, u32[]{:S(2)}, u32[]{:S(2)}) collective-permute-start(s32[512]{0:T(512)S(1)} %get-tuple-element.182), channel_id=1, source_target_pairs={{0,4},{4,8},{8,12},{12,16},{16,20},{20,24},{24,28},{1,5},{5,9},{9,... | collective-permute-start | bytes 6152 | tf_op jit(solution)/shard_map/while/body/eval_jaxpr/ppermute | solution.py:12
  46.2 1.9 %collective-permute-start.2 = (bf16[512,256]{0,1:T(8,128)(2,1)S(1)}, bf16[512,256]{0,1:T(8,128)(2,1)S(1)}, u32[]{:S(2)}, u32[]{:S(2)}) collective-permute-start(bf16[512,256]{0,1:T(8,128)(2,1)S(1)} %get-tuple-element.181), channel_id=1, source_target_pairs={{0,4},{4,8},{8,12},{12,16},{16,20},{20,24},{24,28},{1,5},{5,9},{9,... | collective-permute-start | bytes 786440 | tf_op jit(solution)/shard_map/while/body/eval_jaxpr/ppermute | solution.py:12
  48.1 0.0 collective-permute-done
  48.1 0.2 broadcast_compare_fusion.2
  48.4 0.0 collective-permute-done.1
  48.4 0.0 copy-start
  48.4 2.0 %fusion.42 = (f32[2,4,512]{2,1,0:T(4,128)S(1)}, f32[2,512,512,4]{2,1,3,0:T(8,128)S(1)}) fusion(pred[512,512]{0,1:T(8,128)(4,1)S(1)} %broadcast_compare_fusion.2, bf16[512,2,128,1]{0,2,3,1:T(8,128)(2,1)S(1)} %bitcast.79, bf16[512,2,4,128]{3,0,2,1:T(8,128)(2,1)S(1)} %get-tuple-element.194), kind=kOutput, calls=%fused_computation.4.clone.1 | convolution fusion | flops 543158272 | bytes 9977856 | tf_op jit(solution)/shard_map/while/body/eval_jaxpr/tkgd,skd->kgts/dot_general | solution.py:25
  50.4 1.7 %fusion.43 = f32[2,4,512]{2,1,0:T(4,128)S(1)} fusion(f32[2,512,512,4]{2,1,3,0:T(8,128)S(1)} %get-tuple-element.163, f32[2,4,512]{2,1,0:T(4,128)S(1)} %max.4, pred[512,512]{0,1:T(8,128)(4,1)S(1)} %broadcast_compare_fusion.2), kind=kLoop, calls=%fused_computation.3.clone.1 | loop fusion | flops 8384512 | bytes 8683520 | tf_op jit(solution)/shard_map/while/body/eval_jaxpr/reduce_sum | solution.py:36
  52.2 0.0 collective-permute-done.2
  52.2 0.0 copy-done
  52.2 3.4 %multiply_add_fusion.5 = f32[2,4,512,128]{3,2,1,0:T(8,128)S(1)} fusion(f32[2,4,512,128]{3,2,1,0:T(8,128)S(1)} %copy-done, bf16[512,2,128,1]{0,2,3,1:T(8,128)(2,1)S(1)} %bitcast.83, f32[2,512,512,4]{2,1,3,0:T(8,128)S(1)} %get-tuple-element.163, f32[2,4,512]{2,1,0:T(4,128)S(1)} %max.4, pred[512,512]{0,1:T(8,128)(4,1)S(1)} %broadcast_compare_fusion.2, ...), kind=kOutput, calls=%fused_computation.7.clone.1 | convolution fusion | flops 546308096 | bytes 13139968 | tf_op jit(solution)/shard_map/while/body/eval_jaxpr/kgts,skd->kgtd/dot_general | solution.py:37
  55.6 0.0 copy-start.1
  55.7 1.3 copy-done.1
  57.0 1.9 %copy.36 = f32[2,4,512,128]{2,3,1,0:T(8,128)S(1)} copy(f32[2,4,512,128]{3,2,1,0:T(8,128)} %get-tuple-element.53) | data formatting | bytes 4194304 | tf_op jit(solution)/shard_map/while | solution.py:72
  58.9 1.2 divide_convert_fusion
  60.2 0.0 all-gather.2.cloned.1.call-update
  60.2 83.7 %all-gather.2.cloned.1.call-done = bf16[512,4096]{0,1:T(8,128)(2,1)} async-done(((bf16[512,1024]{0,1:T(8,128)(2,1)}), bf16[512,4096]{0,1:T(8,128)(2,1)}) %all-gather.2.cloned.1.call-update) | async-done | bytes 4194320 | tf_op jit(solution)/shard_map/all_gather | solution.py:83
  143.9 10.1 %convolution_convert_fusion = bf16[512,1024]{1,0:T(8,128)(2,1)} fusion(bf16[512,4096]{0,1:T(8,128)(2,1)} %all-gather.2.cloned.1.call-done, bf16[4096,1024]{1,0:T(8,128)(2,1)} %param.11), kind=kOutput, calls=%fused_computation.22 | convolution fusion | flops 4295491584 | bytes 13631488 | tf_op jit(solution)/shard_map/dot_general | solution.py:82
  (18 shorter events, 0.2 us)
Async XLA Ops:
  6.5 137.4 %all-gather.2.cloned.1.call-start = ((), (), s32[]{:S(2)}) async-start(), calls=%async_computation | async-start | bytes 5242880 | tf_op jit(solution)/shard_map/all_gather | solution.py:83
  21.4 9.1 %collective-permute-start.1 = (bf16[512,256]{0,1:T(8,128)(2,1)S(1)}, bf16[512,256]{0,1:T(8,128)(2,1)S(1)}, u32[]{:S(2)}, u32[]{:S(2)}) collective-permute-start(bf16[512,256]{0,1:T(8,128)(2,1)S(1)} %get-tuple-element.180), channel_id=1, source_target_pairs={{0,4},{4,8},{8,12},{12,16},{16,20},{20,24},{24,28},{1,5},{5,9},{9,... | collective-permute-start | bytes 786440 | tf_op jit(solution)/shard_map/while/body/eval_jaxpr/ppermute | solution.py:12
  23.8 6.4 %collective-permute-start = (s32[512]{0:T(512)S(1)}, s32[512]{0:T(512)S(1)}, u32[]{:S(2)}, u32[]{:S(2)}) collective-permute-start(s32[512]{0:T(512)S(1)} %get-tuple-element.182), channel_id=1, source_target_pairs={{0,4},{4,8},{8,12},{12,16},{16,20},{20,24},{24,28},{1,5},{5,9},{9,... | collective-permute-start | bytes 6152 | tf_op jit(solution)/shard_map/while/body/eval_jaxpr/ppermute | solution.py:12
  28.3 6.0 %collective-permute-start.2 = (bf16[512,256]{0,1:T(8,128)(2,1)S(1)}, bf16[512,256]{0,1:T(8,128)(2,1)S(1)}, u32[]{:S(2)}, u32[]{:S(2)}) collective-permute-start(bf16[512,256]{0,1:T(8,128)(2,1)S(1)} %get-tuple-element.181), channel_id=1, source_target_pairs={{0,4},{4,8},{8,12},{12,16},{16,20},{20,24},{24,28},{1,5},{5,9},{9,... | collective-permute-start | bytes 786440 | tf_op jit(solution)/shard_map/while/body/eval_jaxpr/ppermute | solution.py:12
  30.5 3.9 %copy-start = (f32[2,4,512,128]{3,2,1,0:T(8,128)S(1)}, f32[2,4,512,128]{3,2,1,0:T(8,128)}, u32[]{:S(2)}) copy-start(f32[2,4,512,128]{3,2,1,0:T(8,128)} %get-tuple-element.179) | copy-start | bytes 6291460 | tf_op jit(solution)/shard_map/while
  37.8 1.4 copy-start.1
  39.1 9.2 %collective-permute-start.1 = (bf16[512,256]{0,1:T(8,128)(2,1)S(1)}, bf16[512,256]{0,1:T(8,128)(2,1)S(1)}, u32[]{:S(2)}, u32[]{:S(2)}) collective-permute-start(bf16[512,256]{0,1:T(8,128)(2,1)S(1)} %get-tuple-element.180), channel_id=1, source_target_pairs={{0,4},{4,8},{8,12},{12,16},{16,20},{20,24},{24,28},{1,5},{5,9},{9,... | collective-permute-start | bytes 786440 | tf_op jit(solution)/shard_map/while/body/eval_jaxpr/ppermute | solution.py:12
  42.6 5.5 %collective-permute-start = (s32[512]{0:T(512)S(1)}, s32[512]{0:T(512)S(1)}, u32[]{:S(2)}, u32[]{:S(2)}) collective-permute-start(s32[512]{0:T(512)S(1)} %get-tuple-element.182), channel_id=1, source_target_pairs={{0,4},{4,8},{8,12},{12,16},{16,20},{20,24},{24,28},{1,5},{5,9},{9,... | collective-permute-start | bytes 6152 | tf_op jit(solution)/shard_map/while/body/eval_jaxpr/ppermute | solution.py:12
  46.2 6.0 %collective-permute-start.2 = (bf16[512,256]{0,1:T(8,128)(2,1)S(1)}, bf16[512,256]{0,1:T(8,128)(2,1)S(1)}, u32[]{:S(2)}, u32[]{:S(2)}) collective-permute-start(bf16[512,256]{0,1:T(8,128)(2,1)S(1)} %get-tuple-element.181), channel_id=1, source_target_pairs={{0,4},{4,8},{8,12},{12,16},{16,20},{20,24},{24,28},{1,5},{5,9},{9,... | collective-permute-start | bytes 786440 | tf_op jit(solution)/shard_map/while/body/eval_jaxpr/ppermute | solution.py:12
  48.4 3.9 %copy-start = (f32[2,4,512,128]{3,2,1,0:T(8,128)S(1)}, f32[2,4,512,128]{3,2,1,0:T(8,128)}, u32[]{:S(2)}) copy-start(f32[2,4,512,128]{3,2,1,0:T(8,128)} %get-tuple-element.179) | copy-start | bytes 6291460 | tf_op jit(solution)/shard_map/while
  55.6 1.4 copy-start.1
Sparse Core Ops, SparseCore 0:
  60.3 83.5 all-gather.1
where the time goes:
time: 161 us
  waiting for transfers between devices  83.8 us (52%)
  matrix products  26.4 us (16%)
  starting transfers between devices  17.8 us (11%)
  between operations  13.5 us (8%)
  local copies, waits for them, and re-layouts  11.7 us (7%)
  other arithmetic  7.42 us (5%)
    all_gather x1, waiting for transfers between devices, shards(): lax.all_gather(attended, 'head', axis=1, tiled=True)  83.7 us
    ppermute x6, starting transfers between devices, shifted(): return lax.ppermute(shard, axis, pairs)  17.8 us
    dot_general x3, matrix products, attend(): jnp.einsum('kgts,skd->kgtd', weights.astype(jnp.bfloat16), valued_rows, p...  10.7 us
    dot_general x1, matrix products, shards(): jnp.dot(lax.all_gather(attended, 'head', axis=1, tiled=True), out_weight,...  10.1 us
    dot_general x3, matrix products, attend(): jnp.einsum('tkgd,skd->kgts', grouped_queries, keyed_rows, preferred_eleme...  5.65 us
    reduce_sum x3, other arithmetic, attend(): run_total = run_total * factor + jnp.sum(weights, axis=-1)  5.23 us
    while x4, local copies, waits for them, and re-layouts, shards(): lax.fori_loop(0, reach_shards, turn_step, (softmax_state, (keys, values,...  4.76 us
  transfers between devices with their start and end apart: 7, of which 1 were waited for; matrix products, arithmetic and copies ran while one was open for 5% of the time, Pallas kernels for 0%

commit v1 on v0

--- a/solution.py
+++ b/solution.py
@@ -4,6 +4,15 @@
 from jax.sharding import PartitionSpec as P
 
 HEAD_SIZE = 128
+
+
+def slot_compute(array_here, on_dim):
+    array_here = jnp.moveaxis(array_here, 0, on_dim)
+    taken_in = array_here.shape
+    part_next = array_here.reshape(
+        *taken_in[:on_dim], taken_in[on_dim] * taken_in[on_dim + 1], *taken_in[on_dim + 2 :]
+    )
+    return part_next
 
 
 def shifted(shard, axis, by):
@@ -79,10 +88,22 @@
         .reshape(tok_local, queries.shape[1])
         .astype(jnp.bfloat16)
     )
+
+    def cut_the_marks(local_array, which_axis, out_dim):
+        axis_len = jax.lax.axis_size(which_axis)
+        sides = tuple(((src_i, (src_i + 1) % axis_len) for src_i in range(axis_len)))
+        pages = [local_array]
+        while len(pages) < axis_len:
+            next_value = jax.lax.ppermute(pages[-1], axis_name=which_axis, perm=sides)
+            pages.append(next_value)
+        v_now = jax.lax.axis_index(which_axis)
+        heard = jnp.stack(pages, 0)
+        pages = heard[(v_now - jnp.arange(axis_len)) % axis_len]
+        extra = slot_compute(pages, out_dim)
+        return extra
+
     mixed = jnp.dot(
-        lax.all_gather(attended, "head", axis=1, tiled=True),
-        out_weight,
-        preferred_element_type=jnp.float32,
+        cut_the_marks(attended, "head", 1), out_weight, preferred_element_type=jnp.float32
     )
     return mixed.astype(jnp.bfloat16)
 

time: 161 us -> 153 us (0.950)
  between operations: 13.5 us -> 0.11 us
  local copies, waits for them, and re-layouts: 11.7 us -> 17.4 us
  waiting for transfers between devices: 83.8 us -> 79.3 us
  other arithmetic: 7.42 us -> 9.74 us
    all_gather x1 -> x0, waiting for transfers between devices: 83.7 us -> none  [shards(): lax.all_gather(attended, 'head', axis=1, tiled=True)]
    ppermute x0 -> x3, waiting for transfers between devices: none -> 79.3 us  [cut_the_marks(): next_value = jax.lax.ppermute(pages[-1], axis_name=which_axis, perm=sides)]
    gather x0 -> x1, local copies, waits for them, and re-layouts: none -> 4.97 us  [cut_the_marks(): pages = heard[(v_now - jnp.arange(axis_len)) % axis_len]]
    another operation x2 -> x3, other arithmetic: 0.15 us -> 3.42 us  [the longest x1 3.26 us: cut_the_marks(): heard = jnp.stack(pages, 0)]
    ppermute x0 -> x3, starting transfers between devices: none -> 1.64 us  [cut_the_marks(): next_value = jax.lax.ppermute(pages[-1], axis_name=which_axis, perm=sides)]
  transfers between devices with their start and end apart: 7 -> 9, of which waited for: 1 -> 3; matrix products, arithmetic and copies ran while one was open for 5% -> 5% of each run, Pallas kernels for 0% -> 0%
where the time goes in v1:
time: 153 us
  waiting for transfers between devices  79.3 us (52%)
  matrix products  26.4 us (17%)
  starting transfers between devices  19.4 us (13%)
  local copies, waits for them, and re-layouts  17.4 us (11%)
  other arithmetic  9.74 us (6%)
    ppermute x3, waiting for transfers between devices, cut_the_marks(): next_value = jax.lax.ppermute(pages[-1], axis_name=which_axis, perm=sides)  79.3 us
    ppermute x6, starting transfers between devices, shifted(): return lax.ppermute(shard, axis, pairs)  17.8 us
    dot_general x3, matrix products, attend(): jnp.einsum('kgts,skd->kgtd', weights.astype(jnp.bfloat16), valued_rows, p...  10.7 us
    dot_general x1, matrix products, shards(): jnp.dot(cut_the_marks(attended, 'head', 1), out_weight, preferred_element...  10.1 us
    dot_general x3, matrix products, attend(): jnp.einsum('tkgd,skd->kgts', grouped_queries, keyed_rows, preferred_eleme...  5.65 us
    reduce_sum x3, other arithmetic, attend(): run_total = run_total * factor + jnp.sum(weights, axis=-1)  5.23 us
    gather x1, local copies, waits for them, and re-layouts, cut_the_marks(): pages = heard[(v_now - jnp.arange(axis_len)) % axis_len]  4.97 us
    while x4, local copies, waits for them, and re-layouts, shards(): lax.fori_loop(0, reach_shards, turn_step, (softmax_state, (keys, values,...  4.76 us
  transfers between devices with their start and end apart: 9, of which 3 were waited for; matrix products, arithmetic and copies ran while one was open for 5% of the time, Pallas kernels for 0%

profile of v1, /device:TPU:0, one launch (start us, length us, event | category | flops | bytes accessed | tf_op | source)
XLA Modules:
  0.0 152.7 jit_solution(12929532901409428200)
XLA Ops:
  0.0 0.7 copy.27
  0.8 0.1 reduce
  0.9 0.1 convert_reduce_fusion
  1.0 0.2 fusion.19
  1.2 1.0 reshape.128
  2.2 1.1 copy.33
  3.3 1.7 %reshape.130 = bf16[512,2,128]{2,1,0:T(2,128)(2,1)} reshape(bf16[512,256]{1,0:T(8,128)(2,1)} %param.9) | data formatting | bytes 524288 | tf_op jit(solution)/shard_map/reshape | solution.py:33
  5.1 1.1 copy.34
  6.1 1.5 copy.28
  7.7 0.7 copy.35
  8.3 0.0 copy-start.2
  8.3 1.6 %fusion.12 = (f32[2,4,512]{2,1,0:T(4,128)S(1)}, f32[2,512,512,4]{2,1,3,0:T(8,128)S(1)}) fusion(pred[512,512]{0,1:T(8,128)(4,1)S(1)} %fusion.19, bf16[512,2,4,128]{0,3,2,1:T(8,128)(2,1)S(1)} %bitcast.91, bf16[512,2,128,1]{2,1,0,3:T(2,128)(2,1)S(1)} %bitcast.99), kind=kOutput, calls=%fused_computation.18 | convolution fusion | flops 543158272 | bytes 9977856 | tf_op jit(solution)/shard_map/tkgd,skd->kgts/dot_general | solution.py:34
  9.9 1.7 %fusion.11 = f32[2,4,512]{2,1,0:T(4,128)S(1)} fusion(f32[2,512,512,4]{2,1,3,0:T(8,128)S(1)} %get-tuple-element.98, f32[2,4,512]{2,1,0:T(4,128)S(1)} %broadcast_maximum_fusion, pred[512,512]{0,1:T(8,128)(4,1)S(1)} %fusion.19), kind=kLoop, calls=%fused_computation.17 | loop fusion | flops 8384512 | bytes 8683520 | tf_op jit(solution)/shard_map/reduce_sum | solution.py:45
  11.7 0.0 copy-done.2
  11.7 3.9 %fusion.16 = f32[2,4,512,128]{3,2,1,0:T(8,128)} fusion(f32[2,512,512,4]{2,1,3,0:T(8,128)S(1)} %get-tuple-element.98, f32[2,4,512]{2,1,0:T(4,128)S(1)} %broadcast_maximum_fusion, pred[512,512]{0,1:T(8,128)(4,1)S(1)} %fusion.19, f32[2,4,512]{2,1,0:T(4,128)S(1)} %get-tuple-element.95, bf16[512,2,128,1]{2,1,0,3:T(2,128)(2,1)S(1)} %bitcast.105), kind=kOutput, calls=%fused_computation.23 | convolution fusion | flops 545783808 | bytes 11042816 | tf_op jit(solution)/shard_map/kgts,skd->kgtd/dot_general | solution.py:46
  15.6 35.6 %while.20 = (s32[]{:T(128)}, f32[2,4,512]{2,1,0:T(4,128)S(1)}, f32[2,4,512]{2,1,0:T(4,128)S(1)}, f32[2,4,512,128]{3,2,1,0:T(8,128)}, bf16[512,256]{0,1:T(8,128)(...) while((s32[]{:T(128)}, f32[2,4,512]{2,1,0:T(4,128)S(1)}, ...), condition=%wide.region_7.8_spmd, body=%wide.region_4.7_spmd.sunk | while | flops 1098129408 | bytes 52183316 | solution.py:81
  15.6 2.4 %collective-permute-start.1 = (bf16[512,256]{0,1:T(8,128)(2,1)S(1)}, bf16[512,256]{0,1:T(8,128)(2,1)S(1)}, u32[]{:S(2)}, u32[]{:S(2)}) collective-permute-start(bf16[512,256]{0,1:T(8,128)(2,1)S(1)} %get-tuple-element.180), channel_id=1, source_target_pairs={{0,4},{4,8},{8,12},{12,16},{16,20},{20,24},{24,28},{1,5},{5,9},{9,... | collective-permute-start | bytes 786440 | tf_op jit(solution)/shard_map/while/body/eval_jaxpr/ppermute | solution.py:21
  18.0 4.5 %collective-permute-start = (s32[512]{0:T(512)S(1)}, s32[512]{0:T(512)S(1)}, u32[]{:S(2)}, u32[]{:S(2)}) collective-permute-start(s32[512]{0:T(512)S(1)} %get-tuple-element.182), channel_id=1, source_target_pairs={{0,4},{4,8},{8,12},{12,16},{16,20},{20,24},{24,28},{1,5},{5,9},{9,... | collective-permute-start | bytes 6152 | tf_op jit(solution)/shard_map/while/body/eval_jaxpr/ppermute | solution.py:21
  22.5 1.9 %collective-permute-start.2 = (bf16[512,256]{0,1:T(8,128)(2,1)S(1)}, bf16[512,256]{0,1:T(8,128)(2,1)S(1)}, u32[]{:S(2)}, u32[]{:S(2)}) collective-permute-start(bf16[512,256]{0,1:T(8,128)(2,1)S(1)} %get-tuple-element.181), channel_id=1, source_target_pairs={{0,4},{4,8},{8,12},{12,16},{16,20},{20,24},{24,28},{1,5},{5,9},{9,... | collective-permute-start | bytes 786440 | tf_op jit(solution)/shard_map/while/body/eval_jaxpr/ppermute | solution.py:21
  24.4 0.0 collective-permute-done
  24.4 0.2 broadcast_compare_fusion.2
  24.7 0.0 collective-permute-done.1
  24.7 0.0 copy-start
  24.7 2.0 %fusion.44 = (f32[2,4,512]{2,1,0:T(4,128)S(1)}, f32[2,512,512,4]{2,1,3,0:T(8,128)S(1)}) fusion(pred[512,512]{0,1:T(8,128)(4,1)S(1)} %broadcast_compare_fusion.2, bf16[512,2,128,1]{0,2,3,1:T(8,128)(2,1)S(1)} %bitcast.89, bf16[512,2,4,128]{3,0,2,1:T(8,128)(2,1)S(1)} %get-tuple-element.194), kind=kOutput, calls=%fused_computation.5.clone.1 | convolution fusion | flops 543158272 | bytes 9977856 | tf_op jit(solution)/shard_map/while/body/eval_jaxpr/tkgd,skd->kgts/dot_general | solution.py:34
  26.7 1.7 %fusion.45 = f32[2,4,512]{2,1,0:T(4,128)S(1)} fusion(f32[2,512,512,4]{2,1,3,0:T(8,128)S(1)} %get-tuple-element.163, f32[2,4,512]{2,1,0:T(4,128)S(1)} %max.4, pred[512,512]{0,1:T(8,128)(4,1)S(1)} %broadcast_compare_fusion.2), kind=kLoop, calls=%fused_computation.4.clone.1 | loop fusion | flops 8384512 | bytes 8683520 | tf_op jit(solution)/shard_map/while/body/eval_jaxpr/reduce_sum | solution.py:45
  28.5 0.0 collective-permute-done.2
  28.5 0.0 copy-done
  28.5 3.4 %multiply_add_fusion.5 = f32[2,4,512,128]{3,2,1,0:T(8,128)S(1)} fusion(f32[2,4,512,128]{3,2,1,0:T(8,128)S(1)} %copy-done, bf16[512,2,128,1]{0,2,3,1:T(8,128)(2,1)S(1)} %bitcast.93, f32[2,512,512,4]{2,1,3,0:T(8,128)S(1)} %get-tuple-element.163, f32[2,4,512]{2,1,0:T(4,128)S(1)} %max.4, pred[512,512]{0,1:T(8,128)(4,1)S(1)} %broadcast_compare_fusion.2, ...), kind=kOutput, calls=%fused_computation.8.clone.1 | convolution fusion | flops 546308096 | bytes 13139968 | tf_op jit(solution)/shard_map/while/body/eval_jaxpr/kgts,skd->kgtd/dot_general | solution.py:46
  31.9 0.0 copy-start.1
  32.0 1.3 copy-done.1
  33.3 3.5 %collective-permute-start.1 = (bf16[512,256]{0,1:T(8,128)(2,1)S(1)}, bf16[512,256]{0,1:T(8,128)(2,1)S(1)}, u32[]{:S(2)}, u32[]{:S(2)}) collective-permute-start(bf16[512,256]{0,1:T(8,128)(2,1)S(1)} %get-tuple-element.180), channel_id=1, source_target_pairs={{0,4},{4,8},{8,12},{12,16},{16,20},{20,24},{24,28},{1,5},{5,9},{9,... | collective-permute-start | bytes 786440 | tf_op jit(solution)/shard_map/while/body/eval_jaxpr/ppermute | solution.py:21
  36.8 3.5 %collective-permute-start = (s32[512]{0:T(512)S(1)}, s32[512]{0:T(512)S(1)}, u32[]{:S(2)}, u32[]{:S(2)}) collective-permute-start(s32[512]{0:T(512)S(1)} %get-tuple-element.182), channel_id=1, source_target_pairs={{0,4},{4,8},{8,12},{12,16},{16,20},{20,24},{24,28},{1,5},{5,9},{9,... | collective-permute-start | bytes 6152 | tf_op jit(solution)/shard_map/while/body/eval_jaxpr/ppermute | solution.py:21
  40.3 1.9 %collective-permute-start.2 = (bf16[512,256]{0,1:T(8,128)(2,1)S(1)}, bf16[512,256]{0,1:T(8,128)(2,1)S(1)}, u32[]{:S(2)}, u32[]{:S(2)}) collective-permute-start(bf16[512,256]{0,1:T(8,128)(2,1)S(1)} %get-tuple-element.181), channel_id=1, source_target_pairs={{0,4},{4,8},{8,12},{12,16},{16,20},{20,24},{24,28},{1,5},{5,9},{9,... | collective-permute-start | bytes 786440 | tf_op jit(solution)/shard_map/while/body/eval_jaxpr/ppermute | solution.py:21
  42.3 0.0 collective-permute-done
  42.3 0.2 broadcast_compare_fusion.2
  42.5 0.0 collective-permute-done.1
  42.5 0.0 copy-start
  42.6 2.0 %fusion.44 = (f32[2,4,512]{2,1,0:T(4,128)S(1)}, f32[2,512,512,4]{2,1,3,0:T(8,128)S(1)}) fusion(pred[512,512]{0,1:T(8,128)(4,1)S(1)} %broadcast_compare_fusion.2, bf16[512,2,128,1]{0,2,3,1:T(8,128)(2,1)S(1)} %bitcast.89, bf16[512,2,4,128]{3,0,2,1:T(8,128)(2,1)S(1)} %get-tuple-element.194), kind=kOutput, calls=%fused_computation.5.clone.1 | convolution fusion | flops 543158272 | bytes 9977856 | tf_op jit(solution)/shard_map/while/body/eval_jaxpr/tkgd,skd->kgts/dot_general | solution.py:34
  44.6 1.7 %fusion.45 = f32[2,4,512]{2,1,0:T(4,128)S(1)} fusion(f32[2,512,512,4]{2,1,3,0:T(8,128)S(1)} %get-tuple-element.163, f32[2,4,512]{2,1,0:T(4,128)S(1)} %max.4, pred[512,512]{0,1:T(8,128)(4,1)S(1)} %broadcast_compare_fusion.2), kind=kLoop, calls=%fused_computation.4.clone.1 | loop fusion | flops 8384512 | bytes 8683520 | tf_op jit(solution)/shard_map/while/body/eval_jaxpr/reduce_sum | solution.py:45
  46.4 0.0 collective-permute-done.2
  46.4 0.0 copy-done
  46.4 3.4 %multiply_add_fusion.5 = f32[2,4,512,128]{3,2,1,0:T(8,128)S(1)} fusion(f32[2,4,512,128]{3,2,1,0:T(8,128)S(1)} %copy-done, bf16[512,2,128,1]{0,2,3,1:T(8,128)(2,1)S(1)} %bitcast.93, f32[2,512,512,4]{2,1,3,0:T(8,128)S(1)} %get-tuple-element.163, f32[2,4,512]{2,1,0:T(4,128)S(1)} %max.4, pred[512,512]{0,1:T(8,128)(4,1)S(1)} %broadcast_compare_fusion.2, ...), kind=kOutput, calls=%fused_computation.8.clone.1 | convolution fusion | flops 546308096 | bytes 13139968 | tf_op jit(solution)/shard_map/while/body/eval_jaxpr/kgts,skd->kgtd/dot_general | solution.py:46
  49.8 0.0 copy-start.1
  49.9 1.3 copy-done.1
  51.2 1.9 %copy.36 = f32[2,4,512,128]{2,3,1,0:T(8,128)S(1)} copy(f32[2,4,512,128]{3,2,1,0:T(8,128)} %get-tuple-element.53) | data formatting | bytes 4194304 | tf_op jit(solution)/shard_map/while | solution.py:81
  53.1 0.3 divide_convert_fusion
  53.4 1.6 %collective-permute-start.3 = (bf16[512,1024]{0,1:T(8,128)(2,1)S(1)}, bf16[512,1024]{0,1:T(8,128)(2,1)S(1)}, u32[]{:S(2)}, u32[]{:S(2)}) collective-permute-start(bf16[512,1024]{0,1:T(8,128)(2,1)S(1)} %bitcast.95), channel_id=1, source_target_pairs={{0,1},{1,2},{2,3},{3,0},{4,5},{5,6},{6,7},{7,4},{8,9},{9,10},{10,1... | collective-permute-start | bytes 3145736 | tf_op jit(solution)/shard_map/ppermute | solution.py:97
  55.0 24.7 %collective-permute-done.3 = bf16[512,1024]{0,1:T(8,128)(2,1)S(1)} collective-permute-done((bf16[512,1024]{0,1:T(8,128)(2,1)S(1)}, bf16[512,1024]{0,1:T(8,128)(2,1)S(1)}, u32[]{:S(2)}, u32[]{:S(2)}) %collective-permute-start.3) | collective-permute-done | bytes 1048608 | tf_op jit(solution)/shard_map/ppermute | solution.py:97
  79.7 0.0 collective-permute-start.4
  79.7 27.4 %collective-permute-done.4 = bf16[512,1024]{0,1:T(8,128)(2,1)S(1)} collective-permute-done((bf16[512,1024]{0,1:T(8,128)(2,1)S(1)}, bf16[512,1024]{0,1:T(8,128)(2,1)S(1)}, u32[]{:S(2)}, u32[]{:S(2)}) %collective-permute-start.4) | collective-permute-done | bytes 1048608 | tf_op jit(solution)/shard_map/ppermute | solution.py:97
  107.1 0.0 collective-permute-start.5
  107.1 27.2 %collective-permute-done.5 = bf16[512,1024]{0,1:T(8,128)(2,1)} collective-permute-done((bf16[512,1024]{0,1:T(8,128)(2,1)S(1)}, bf16[512,1024]{0,1:T(8,128)(2,1)}, u32[]{:S(2)}, u32[]{:S(2)}) %collective-permute-start.5) | collective-permute-done | bytes 1048608 | tf_op jit(solution)/shard_map/ppermute | solution.py:97
  134.3 3.3 %pad_maximum_fusion = bf16[4,512,1024]{1,2,0:T(8,128)(2,1)} fusion(bf16[1,512,1024]{1,2,0:T(8,128)(2,1)} %bitcast.15, bf16[1,512,1024]{1,2,0:T(8,128)(2,1)S(1)} %bitcast.101, bf16[1,512,1024]{1,2,0:T(8,128)(2,1)S(1)} %bitcast.100, bf16[1,512,1024]{1,2,0:T(8,128)(2,1)S(1)} %bitcast.96), kind=kLoop, calls=%fused_computation.19 | loop fusion | flops 6291456 | bytes 8388608 | tf_op jit(solution)/shard_map/stack | solution.py:100
  137.6 5.0 %gather_fusion = bf16[4,512,1024]{1,2,0:T(8,128)(2,1)} fusion(bf16[4,512,1024]{1,2,0:T(8,128)(2,1)} %pad_maximum_fusion, s32[1024]{0:T(1024)S(1)} %pad_clamp_fusion), kind=kCustom, calls=%fused_computation | custom fusion | bytes 8388624 | tf_op jit(solution)/shard_map/gather | solution.py:101
  142.5 10.1 %convolution_convert_fusion = bf16[512,1024]{1,0:T(8,128)(2,1)} fusion(bf16[512,4096]{0,1:T(8,128)(2,1)} %bitcast.94, bf16[4096,1024]{1,0:T(8,128)(2,1)} %param.11), kind=kOutput, calls=%fused_computation.24 | convolution fusion | flops 4295491584 | bytes 13631488 | tf_op jit(solution)/shard_map/dot_general | solution.py:105
  (20 shorter events, 0.2 us)
Async XLA Ops:
  8.3 3.4 %copy-start.2 = (bf16[512,2,128]{2,1,0:T(2,128)(2,1)S(1)}, bf16[512,2,128]{2,1,0:T(2,128)(2,1)}, u32[]{:S(2)}) copy-start(bf16[512,2,128]{2,1,0:T(2,128)(2,1)} %reshape.130) | copy-start | bytes 786436
  15.6 9.1 %collective-permute-start.1 = (bf16[512,256]{0,1:T(8,128)(2,1)S(1)}, bf16[512,256]{0,1:T(8,128)(2,1)S(1)}, u32[]{:S(2)}, u32[]{:S(2)}) collective-permute-start(bf16[512,256]{0,1:T(8,128)(2,1)S(1)} %get-tuple-element.180), channel_id=1, source_target_pairs={{0,4},{4,8},{8,12},{12,16},{16,20},{20,24},{24,28},{1,5},{5,9},{9,... | collective-permute-start | bytes 786440 | tf_op jit(solution)/shard_map/while/body/eval_jaxpr/ppermute | solution.py:21
  18.0 6.4 %collective-permute-start = (s32[512]{0:T(512)S(1)}, s32[512]{0:T(512)S(1)}, u32[]{:S(2)}, u32[]{:S(2)}) collective-permute-start(s32[512]{0:T(512)S(1)} %get-tuple-element.182), channel_id=1, source_target_pairs={{0,4},{4,8},{8,12},{12,16},{16,20},{20,24},{24,28},{1,5},{5,9},{9,... | collective-permute-start | bytes 6152 | tf_op jit(solution)/shard_map/while/body/eval_jaxpr/ppermute | solution.py:21
  22.5 6.0 %collective-permute-start.2 = (bf16[512,256]{0,1:T(8,128)(2,1)S(1)}, bf16[512,256]{0,1:T(8,128)(2,1)S(1)}, u32[]{:S(2)}, u32[]{:S(2)}) collective-permute-start(bf16[512,256]{0,1:T(8,128)(2,1)S(1)} %get-tuple-element.181), channel_id=1, source_target_pairs={{0,4},{4,8},{8,12},{12,16},{16,20},{20,24},{24,28},{1,5},{5,9},{9,... | collective-permute-start | bytes 786440 | tf_op jit(solution)/shard_map/while/body/eval_jaxpr/ppermute | solution.py:21
  24.7 3.9 %copy-start = (f32[2,4,512,128]{3,2,1,0:T(8,128)S(1)}, f32[2,4,512,128]{3,2,1,0:T(8,128)}, u32[]{:S(2)}) copy-start(f32[2,4,512,128]{3,2,1,0:T(8,128)} %get-tuple-element.179) | copy-start | bytes 6291460 | tf_op jit(solution)/shard_map/while
  31.9 1.4 copy-start.1
  33.3 9.2 %collective-permute-start.1 = (bf16[512,256]{0,1:T(8,128)(2,1)S(1)}, bf16[512,256]{0,1:T(8,128)(2,1)S(1)}, u32[]{:S(2)}, u32[]{:S(2)}) collective-permute-start(bf16[512,256]{0,1:T(8,128)(2,1)S(1)} %get-tuple-element.180), channel_id=1, source_target_pairs={{0,4},{4,8},{8,12},{12,16},{16,20},{20,24},{24,28},{1,5},{5,9},{9,... | collective-permute-start | bytes 786440 | tf_op jit(solution)/shard_map/while/body/eval_jaxpr/ppermute | solution.py:21
  36.8 5.5 %collective-permute-start = (s32[512]{0:T(512)S(1)}, s32[512]{0:T(512)S(1)}, u32[]{:S(2)}, u32[]{:S(2)}) collective-permute-start(s32[512]{0:T(512)S(1)} %get-tuple-element.182), channel_id=1, source_target_pairs={{0,4},{4,8},{8,12},{12,16},{16,20},{20,24},{24,28},{1,5},{5,9},{9,... | collective-permute-start | bytes 6152 | tf_op jit(solution)/shard_map/while/body/eval_jaxpr/ppermute | solution.py:21
  40.3 6.0 %collective-permute-start.2 = (bf16[512,256]{0,1:T(8,128)(2,1)S(1)}, bf16[512,256]{0,1:T(8,128)(2,1)S(1)}, u32[]{:S(2)}, u32[]{:S(2)}) collective-permute-start(bf16[512,256]{0,1:T(8,128)(2,1)S(1)} %get-tuple-element.181), channel_id=1, source_target_pairs={{0,4},{4,8},{8,12},{12,16},{16,20},{20,24},{24,28},{1,5},{5,9},{9,... | collective-permute-start | bytes 786440 | tf_op jit(solution)/shard_map/while/body/eval_jaxpr/ppermute | solution.py:21
  42.5 3.9 %copy-start = (f32[2,4,512,128]{3,2,1,0:T(8,128)S(1)}, f32[2,4,512,128]{3,2,1,0:T(8,128)}, u32[]{:S(2)}) copy-start(f32[2,4,512,128]{3,2,1,0:T(8,128)} %get-tuple-element.179) | copy-start | bytes 6291460 | tf_op jit(solution)/shard_map/while
  49.8 1.4 copy-start.1
  53.4 26.3 %collective-permute-start.3 = (bf16[512,1024]{0,1:T(8,128)(2,1)S(1)}, bf16[512,1024]{0,1:T(8,128)(2,1)S(1)}, u32[]{:S(2)}, u32[]{:S(2)}) collective-permute-start(bf16[512,1024]{0,1:T(8,128)(2,1)S(1)} %bitcast.95), channel_id=1, source_target_pairs={{0,1},{1,2},{2,3},{3,0},{4,5},{5,6},{6,7},{7,4},{8,9},{9,10},{10,1... | collective-permute-start | bytes 3145736 | tf_op jit(solution)/shard_map/ppermute | solution.py:97
  79.7 27.4 %collective-permute-start.4 = (bf16[512,1024]{0,1:T(8,128)(2,1)S(1)}, bf16[512,1024]{0,1:T(8,128)(2,1)S(1)}, u32[]{:S(2)}, u32[]{:S(2)}) collective-permute-start(bf16[512,1024]{0,1:T(8,128)(2,1)S(1)} %collective-permute-done.3), channel_id=1, source_target_pairs={{0,1},{1,2},{2,3},{3,0},{4,5},{5,6},{6,7},{7,4},{8,9},{9,10},{10,1... | collective-permute-start | bytes 3145736 | tf_op jit(solution)/shard_map/ppermute | solution.py:97
  107.1 27.2 %collective-permute-start.5 = (bf16[512,1024]{0,1:T(8,128)(2,1)S(1)}, bf16[512,1024]{0,1:T(8,128)(2,1)}, u32[]{:S(2)}, u32[]{:S(2)}) collective-permute-start(bf16[512,1024]{0,1:T(8,128)(2,1)S(1)} %collective-permute-done.4), channel_id=1, source_target_pairs={{0,1},{1,2},{2,3},{3,0},{4,5},{5,6},{6,7},{7,4},{8,9},{9,10},{10,1... | collective-permute-start | bytes 3145736 | tf_op jit(solution)/shard_map/ppermute | solution.py:97
